TPU v7x, 128 devices: a whole 4x4x4 slice. The times are simulated.
128 devices in a mesh: seq: 32 (over z, y, core), head: 4 (over x).
Axes of the slice: x: 4, y: 4, z: 4, core: 2. Of those that a mesh axis runs over, the one named last changes fastest.
Arguments:
- tokens: bfloat16 [32768, 2048], P('seq'), may hold values from -6 to 6
- w_query: bfloat16 [2048, 2048], P(None, 'head'), may hold values from -0.125 to 0.125
- w_key: bfloat16 [2048, 2048], P(None, 'head'), may hold values from -0.125 to 0.125
- w_value: bfloat16 [2048, 2048], P(None, 'head'), may hold values from -0.125 to 0.125
- omega: float32 [128, 256], replicated, may hold values from -5 to 5
- w_out: bfloat16 [2048, 2048], P('head'), may hold values from -0.125 to 0.125
Outputs:
- mixed: bfloat16 [32768, 2048], P(('seq', 'head'))
All inputs are finite; a program needn't handle non-finite values.
Results may differ from a plain program's by a relative error of at most 0.0063.
Values may be sent and summed in bfloat16 or wider, within the bound.
A program may use at most 128 MiB of HBM per device.

v0:
```python
import math

import jax
import jax.numpy as jnp
from jax import lax
from jax.sharding import PartitionSpec as P

BLOCK = 512


highest_precision = lax.Precision.HIGHEST
stabilizer = 0.001


def prefix(value, axis, join, neutral):
    count, mine = (lax.axis_size(axis), lax.axis_index(axis))
    pieces = jax.tree.map(lambda part: lax.all_gather(part, axis), value)
    so_far = jax.tree.map(
        lambda part, zero: jnp.full_like(part, 0) + jnp.asarray(zero, part.dtype), value, neutral
    )

    def turn(position, so_far):
        longer = join(so_far, jax.tree.map(lambda part: part[position], pieces))
        return jax.tree.map(lambda new, old: jnp.where(position < mine, new, old), longer, so_far)

    return lax.fori_loop(0, count - 1, turn, so_far)


def feature_map(values, omega):
    head_size = omega.shape[0]
    scaled = values * head_size ** (-0.25)
    projected = jnp.einsum("thd,dm->thm", scaled, omega, precision=highest_precision)
    half_square = 0.5 * jnp.sum(scaled * scaled, axis=-1, keepdims=True)
    return ((jnp.exp(projected - half_square) + stabilizer) / math.sqrt(omega.shape[1])).astype(
        jnp.bfloat16
    )


def add_pair(earlier, later):
    return (earlier[0] + later[0], earlier[1] + later[1])


def shards(tokens, w_query, w_key, w_value, omega, w_out):
    tok_rows = tokens.shape[0]
    head_size = omega.shape[0]
    local_heads = w_query.shape[1] // head_size
    query = jnp.dot(tokens, w_query, preferred_element_type=jnp.float32).reshape(
        tok_rows, local_heads, head_size
    )
    key = jnp.dot(tokens, w_key, preferred_element_type=jnp.float32).reshape(
        tok_rows, local_heads, head_size
    )
    value = (
        jnp.dot(tokens, w_value, preferred_element_type=jnp.float32)
        .astype(jnp.bfloat16)
        .reshape(tok_rows, local_heads, head_size)
    )
    query_feat = feature_map(query, omega)
    key_feat = feature_map(key, omega)
    block_count = tok_rows // BLOCK
    block_states = []
    block_norms = []
    for block_index in range(block_count):
        block_keys = key_feat[block_index * BLOCK : (block_index + 1) * BLOCK]
        block_values = value[block_index * BLOCK : (block_index + 1) * BLOCK]
        block_states.append(
            jnp.einsum("xtv,xte->tve", block_keys, block_values, preferred_element_type=jnp.float32)
        )
        block_norms.append(jnp.sum(block_keys, axis=0, dtype=jnp.float32))
    state_total = block_states[0]
    norm_total = block_norms[0]
    block_index = 1
    state_total = state_total + block_states[block_index]
    norm_total = norm_total + block_norms[block_index]
    zero_state = jnp.zeros_like(state_total)
    zero_norm = jnp.zeros_like(norm_total)
    state_prefix, norm_prefix = prefix(
        (state_total, norm_total), "seq", add_pair, (zero_state, zero_norm)
    )
    causal = jnp.arange(BLOCK)[:, None] >= jnp.arange(BLOCK)[None, :]
    cumulative_state = state_prefix
    running_norm = norm_prefix
    outputs = []
    for block_index in range(block_count):
        query_block = query_feat[block_index * BLOCK : (block_index + 1) * BLOCK]
        block_keys = key_feat[block_index * BLOCK : (block_index + 1) * BLOCK]
        block_values = value[block_index * BLOCK : (block_index + 1) * BLOCK]
        scores = jnp.einsum(
            "thm,shm->hts", query_block, block_keys, preferred_element_type=jnp.float32
        )
        scores = jnp.where(causal[None], scores, jnp.float32(0.0))
        query_features = query_block.astype(jnp.float32)
        denom = jnp.sum(scores, axis=-1).T + jnp.einsum(
            "thm,hm->th", query_features, running_norm, precision=highest_precision
        )
        weights = scores.astype(jnp.bfloat16)
        numerator = jnp.einsum(
            "hts,shd->thd", weights, block_values, preferred_element_type=jnp.float32
        )
        numerator = numerator + jnp.einsum(
            "crx,rxs->crs", query_features, cumulative_state, precision=highest_precision
        )
        outputs.append((numerator / denom[..., None]).astype(jnp.bfloat16))
        cumulative_state = cumulative_state + block_states[block_index]
        running_norm = running_norm + block_norms[block_index]
    attention = jnp.concatenate(outputs, axis=0).reshape(tok_rows, local_heads * head_size)
    mixed = lax.psum_scatter(
        jnp.dot(attention, w_out, preferred_element_type=jnp.float32),
        "head",
        scatter_dimension=0,
        tiled=True,
    )
    return mixed.astype(jnp.bfloat16)


def solution(mesh):
    placed = (
        P("seq", None),
        P(None, "head"),
        P(None, "head"),
        P(None, "head"),
        P(),
        P("head", None),
    )
    return jax.shard_map(
        shards, mesh=mesh, in_specs=placed, out_specs=P(("seq", "head"), None), check_vma=False
    )
```

profile of v0, /device:TPU:1, one launch (start us, length us, event | category | flops | bytes accessed | tf_op | source)
XLA Modules:
  0.0 241.3 jit_solution(11198362902272242694)
XLA Ops:
  6.5 5.4 %multiply_reduce_fusion = (f32[1024,4]{0,1:T(4,128)S(1)}, f32[1024,512]{0,1:T(8,128)S(1)}) fusion(bf16[1024,2048]{1,0:T(8,128)(2,1)} %param.8, bf16[2048,512]{1,0:T(8,128)(2,1)} %param.10), kind=kOutput, calls=%fused_computation.14 | convolution fusion | flops 2149052416 | bytes 8404992 | tf_op jit(solution)/shard_map/dot_general | solution.py:50
  12.0 2.4 %convolution_convert_fusion = bf16[1024,512]{0,1:T(8,128)(2,1)S(1)} fusion(bf16[1024,2048]{1,0:T(8,128)(2,1)S(1)} %copy-done.12, bf16[2048,512]{1,0:T(8,128)(2,1)S(1)} %copy-done.13), kind=kOutput, calls=%fused_computation.20 | convolution fusion | flops 2148007936 | bytes 7340032 | tf_op jit(solution)/shard_map/dot_general | solution.py:54
  15.3 4.7 %multiply_convert_fusion = bf16[1024,4,256]{2,0,1:T(8,128)(2,1)S(1)} fusion(f32[1024,4,128]{0,2,1:T(8,128)S(1)} %bitcast.72, f32[1024,4]{0,1:T(4,128)S(1)} %broadcast_multiply_fusion, f32[128,256]{1,0:T(8,128)S(1)} %copy-done.15), kind=kOutput, calls=%fused_computation.2 | convolution fusion | flops 1614807040 | bytes 4341760 | tf_op jit(solution)/shard_map/thd,dm->thm/dot_general | solution.py:32
  21.4 1.3 convolution_add_fusion
  22.8 2.0 convert_reduce_fusion
  24.8 27.5 %all-gather.2 = f32[32,4,256]{2,1,0:T(4,128)S(1)} all-gather(f32[1,4,256]{2,1,0:T(4,128)S(1)} %add_bitcast_fusion.1), channel_id=3, replica_groups=mesh['seq'=32,'head'=4] {'seq'}, dimensions={0}, use_global_device_ids=true | all-gather | bytes 135168 | tf_op jit(solution)/shard_map/all_gather | solution.py:17
  52.4 4.7 %multiply_reduce_fusion.1 = (f32[1024,4]{0,1:T(4,128)S(1)}, f32[1024,512]{0,1:T(8,128)S(1)}) fusion(bf16[1024,2048]{1,0:T(8,128)(2,1)} %param.8, bf16[2048,512]{1,0:T(8,128)(2,1)S(1)} %copy-done.14), kind=kOutput, calls=%fused_computation.15 | convolution fusion | flops 2149052416 | bytes 8404992 | tf_op jit(solution)/shard_map/dot_general | solution.py:47
  57.1 4.9 %multiply_convert_fusion.1 = bf16[1024,4,256]{2,0,1:T(8,128)(2,1)S(1)} fusion(f32[1024,4,128]{0,2,1:T(8,128)S(1)} %bitcast.73, f32[1024,4]{0,1:T(4,128)S(1)} %broadcast_multiply_fusion.1, f32[128,256]{1,0:T(8,128)S(1)} %copy-done.16), kind=kOutput, calls=%fused_computation.3 | convolution fusion | flops 1614807040 | bytes 4341760 | tf_op jit(solution)/shard_map/thd,dm->thm/dot_general | solution.py:32
  63.4 1.9 copy-done.5
  65.3 3.0 %select_reduce_fusion.1 = (f32[4,512]{1,0:T(4,128)S(1)}, f32[4,512]{1,0:T(4,128)}, bf16[4,512,512]{1,2,0:T(8,128)(2,1)}) fusion(pred[512,512]{0,1:T(8,128)(4,1)S(1)} %iota_compare_fusion, f32[4,512,512]{1,2,0:T(8,128)S(1)} %fusion.18, bf16[1024,4,256]{2,0,1:T(8,128)(2,1)S(1)} %copy-done.4, bf16[1024,4,256]{2,0,1:T(8,128)(2,1)S(1)} %multiply_convert_fusion.1), kind=kOutput, calls=%fused_computation.6 | convolution fusion | flops 542109696 | bytes 8667136 | tf_op jit(solution)/shard_map/thm,shm->hts/dot_general | solution.py:88
  68.3 30.8 %all-gather.5.cloned.1.call-done = f32[128,256,128]{2,1,0:T(8,128)} async-done(((f32[4,256,128]{2,1,0:T(8,128)}), f32[128,256,128]{2,1,0:T(8,128)}) %all-gather.5.cloned.1.call-update) | async-done | bytes 16777232 | tf_op jit(solution)/shard_map/all_gather | solution.py:17
  99.2 39.1 %while.16 = (s32[]{:T(128)}, f32[4,256,128]{2,1,0:T(8,128)S(1)}, f32[4,256]{1,0:T(4,128)S(1)}, s32[]{:T(128)}, f32[32,4,256,128]{3,2,1,0:T(8,128)}, /*index=5*/f32[32,4,256]{2,1,0:T(4,128)S(1)}, s32[]{:T(128)}, s32[]{:T(128)}) while((s32[]{:T(128)}, f32[4,256,128]{2,1,0:T(8,128)S(1)}, f32[4,256]{1,0:T(4,128)S(1)}, s32[]{:T(128)}, ...), condition=%wide.region_5.6_spmd.clone, body=%wide.region_4.5_spmd.clone.sunk | while | flops 396292 | bytes 1585267 | solution.py:26
  101.7 1.2 add_select_fusion.4
  102.9 1.2 add_select_fusion.4
  104.2 1.2 add_select_fusion.4
  106.7 1.2 add_select_fusion.4
  108.0 1.2 add_select_fusion.4
  109.3 1.2 add_select_fusion.4
  111.8 1.2 add_select_fusion.4
  138.3 2.6 %fusion.28 = f32[4,128,512]{2,1,0:T(8,128)S(1)} fusion(f32[4,256,128]{2,1,0:T(8,128)S(1)} %get-tuple-element.115, bf16[1024,4,256]{2,0,1:T(8,128)(2,1)} %copy-done.1), kind=kOutput, calls=%fused_computation.46 | convolution fusion | flops 805306368 | bytes 2621440 | tf_op jit(solution)/shard_map/crx,rxs->crs/dot_general | solution.py:100
  140.9 1.2 fusion.16
  146.5 5.6 %fusion.41 = f32[1024,2048]{1,0:T(8,128)} fusion(bf16[1024,512]{0,1:T(8,128)(2,1)S(1)} %bitcast.69, bf16[512,2048]{1,0:T(8,128)(2,1)S(1)} %copy-done), kind=kOutput, calls=%fused_computation.65 | convolution fusion | flops 2147483648 | bytes 11534336 | tf_op jit(solution)/shard_map/dot_general | solution.py:108
  152.2 79.6 %reduce-scatter.2.cloned.1.call-done = f32[256,2048]{1,0:T(8,128)} async-done(((f32[1024,2048]{1,0:T(8,128)}), f32[256,2048]{1,0:T(8,128)}) %reduce-scatter.2.cloned.1.call-update) | async-done | bytes 2097168 | tf_op jit(solution)/shard_map/reduce_scatter | solution.py:107
  231.8 2.7 %convert_element_type.41 = bf16[256,2048]{1,0:T(8,128)(2,1)} convert(f32[256,2048]{1,0:T(8,128)} %reduce-scatter.2.cloned.1.call-done) | non-fusion elementwise | flops 524288 | bytes 3145728 | tf_op jit(solution)/shard_map/convert_element_type | solution.py:113
  (110 shorter events, 37.7 us)
Async XLA Ops:
  6.5 140.0 %copy-start = (bf16[512,2048]{1,0:T(8,128)(2,1)S(1)}, bf16[512,2048]{1,0:T(8,128)(2,1)}, u32[]{:S(2)}) copy-start(bf16[512,2048]{1,0:T(8,128)(2,1)} %param.13) | copy-start | bytes 6291460
  6.5 92.6 %all-gather.5.cloned.1.call-start = ((), (), s32[]{:S(2)}) async-start(), calls=%async_computation.2 | async-start | bytes 17301504 | tf_op jit(solution)/shard_map/all_gather | solution.py:17
  6.5 5.4 %copy-start.12 = (bf16[1024,2048]{1,0:T(8,128)(2,1)S(1)}, bf16[1024,2048]{1,0:T(8,128)(2,1)}, u32[]{:S(2)}) copy-start(bf16[1024,2048]{1,0:T(8,128)(2,1)} %param.8) | copy-start | bytes 12582916
  6.5 5.4 %copy-start.13 = (bf16[2048,512]{1,0:T(8,128)(2,1)S(1)}, bf16[2048,512]{1,0:T(8,128)(2,1)}, u32[]{:S(2)}) copy-start(bf16[2048,512]{1,0:T(8,128)(2,1)} %param.11) | copy-start | bytes 6291460
  14.4 0.9 copy-start.15
  14.5 5.5 %copy-start.9 = (bf16[512,512]{0,1:T(8,128)(2,1)}, bf16[512,512]{0,1:T(8,128)(2,1)S(1)}, u32[]{:S(2)}) copy-start(bf16[512,512]{0,1:T(8,128)(2,1)S(1)} %get-tuple-element.155) | copy-start | bytes 1572868
  14.5 6.0 %copy-start.7 = (bf16[512,512]{0,1:T(8,128)(2,1)}, bf16[512,512]{0,1:T(8,128)(2,1)S(1)}, u32[]{:S(2)}) copy-start(bf16[512,512]{0,1:T(8,128)(2,1)S(1)} %get-tuple-element.154) | copy-start | bytes 1572868
  20.0 1.3 copy-start.3
  22.7 209.1 %reduce-scatter.2.cloned.1.call-start = ((), (), s32[]{:S(2)}) async-start(), calls=%async_computation.1 | async-start | bytes 10485760 | tf_op jit(solution)/shard_map/reduce_scatter | solution.py:107
  22.8 29.6 %copy-start.14 = (bf16[2048,512]{1,0:T(8,128)(2,1)S(1)}, bf16[2048,512]{1,0:T(8,128)(2,1)}, u32[]{:S(2)}) copy-start(bf16[2048,512]{1,0:T(8,128)(2,1)} %param.9) | copy-start | bytes 6291460
  52.4 4.7 %copy-start.16 = (f32[128,256]{1,0:T(8,128)S(1)}, f32[128,256]{1,0:T(8,128)}, u32[]{:S(2)}) copy-start(f32[128,256]{1,0:T(8,128)} %param.12) | copy-start | bytes 393220
  57.1 4.9 %copy-start.4 = (bf16[1024,4,256]{2,0,1:T(8,128)(2,1)S(1)}, bf16[1024,4,256]{2,0,1:T(8,128)(2,1)}, u32[]{:S(2)}) copy-start(bf16[1024,4,256]{2,0,1:T(8,128)(2,1)} %copy-done.3) | copy-start | bytes 6291460
  62.0 1.3 copy-start.1
  63.4 1.9 copy-start.5
  138.3 2.6 %copy-start.2 = (bf16[1024,4,256]{2,0,1:T(8,128)(2,1)S(1)}, bf16[1024,4,256]{2,0,1:T(8,128)(2,1)}, u32[]{:S(2)}) copy-start(bf16[1024,4,256]{2,0,1:T(8,128)(2,1)} %copy-done.1) | copy-start | bytes 6291460
  140.9 3.1 %copy-start.11 = (f32[4,512]{1,0:T(4,128)S(1)}, f32[4,512]{1,0:T(4,128)}, u32[]{:S(2)}) copy-start(f32[4,512]{1,0:T(4,128)} %get-tuple-element.141) | copy-start | bytes 24580
  140.9 3.2 %copy-start.6 = (f32[4,512,512]{1,2,0:T(8,128)S(1)}, f32[4,512,512]{1,2,0:T(8,128)}, u32[]{:S(2)}) copy-start(f32[4,512,512]{1,2,0:T(8,128)} %copy-done.5) | copy-start | bytes 12582916
  140.9 3.2 %copy-start.8 = (bf16[512,512]{0,1:T(8,128)(2,1)S(1)}, bf16[512,512]{0,1:T(8,128)(2,1)}, u32[]{:S(2)}) copy-start(bf16[512,512]{0,1:T(8,128)(2,1)} %copy-done.7) | copy-start | bytes 1572868
  144.1 1.0 copy-start.10
  144.1 1.8 copy-start.17
Sparse Core Ops, SparseCore 0:
  22.8 76.3 all-gather.4
  152.3 79.4 reduce-scatter.1
where the time goes:
time: 243 us; the launch traced here: 241 us
  waiting for transfers between devices  110 us (45%)
  other arithmetic  43.2 us (18%)
  matrix products  40.1 us (17%)
  blocking collectives  27.5 us (11%)
  between operations  13.8 us (6%)
  local copies, waits for them, and re-layouts  5.4 us (2%)
    reduce_scatter x1, waiting for transfers between devices, shards(): lax.psum_scatter(jnp.dot(attention, w_out, preferred_element_type=jnp.flo...  79.6 us
    select_n x62, other arithmetic, turn(): jnp.where(position < mine, new, old)  38.3 us
    all_gather x1, waiting for transfers between devices, prefix(): pieces = jax.tree.map(lambda part: lax.all_gather(part, axis), value)  30.8 us
    all_gather x1, blocking collectives, prefix(): pieces = jax.tree.map(lambda part: lax.all_gather(part, axis), value)  27.5 us
    dot_general x2, matrix products, feature_map(): jnp.einsum('thd,dm->thm', scaled, omega, precision=highest_precision)  9.57 us
    dot_general x1, matrix products, shards(): jnp.dot(attention, w_out, preferred_element_type=jnp.float32)  5.62 us
    dot_general x1, matrix products, shards(): jnp.dot(tokens, w_key, preferred_element_type=jnp.float32)  5.4 us
    unnamed x36, local copies, waits for them, and re-layouts  5.32 us
  transfers between devices with their start and end apart: 2, of which 2 were waited for; matrix products, arithmetic and copies ran while one was open for 6% of the time, Pallas kernels for 0%

commit v1 on v0

v1 whole, which is shorter than its diff:
```python
import functools

import jax
import jax.numpy as jnp
from jax import lax
from jax.experimental import pallas as pl
from jax.experimental.pallas import tpu as pltpu
from jax.sharding import PartitionSpec as P

MESH = pl.DeviceIdType.MESH
BF, F32 = jnp.bfloat16, jnp.float32
LOG2E = 1.4426950408889634
CHUNK = 256
NORM = 16
DIRECT = 64

NT = (((1,), (1,)), ((), ()))


def dot(a, b):
    return jnp.dot(a, b, preferred_element_type=F32)


def dot_nt(a, b):
    return lax.dot_general(a, b, NT, preferred_element_type=F32)


def widen(state):
    norm = state[128:]
    return jnp.concatenate([state[:128]] + [norm] * (128 // NORM), axis=0)


def kernel(
    tok, wq, wk, wv, om, wo, out,
    tokv, wqv, wkv, wvv, wof, kf, qf, vv, omw, run, sloc, acc, res,
    sx, r0, ma, ra, ma2, ra2, mb, rb, mb2, rb2, pa, ua, pb, ps, pf, atts, attb,
    lsem, s0, q0, s1a, q1a, s1b, q1b, s2a, q2a, s2b, q2b, s3, q3, sA, qA,
    wsd, wqd, wsx, wqx, wsy, wqy, wsp, wqp,
):
    seq, x = lax.axis_index("seq"), lax.axis_index("head")
    z, y, c = lax.div(seq, 8), lax.rem(lax.div(seq, 2), 4), lax.rem(seq, 2)

    def ahead(v, o):
        return lax.rem(v + o, 4)

    def dev(z_, y_, c_, x_):
        return {"seq": z_ * 8 + y_ * 2 + c_, "head": x_}

    partner = dev(z, y, 1 - c, x)
    ydev = [dev(z, ahead(y, o), c, x) for o in (1, 2, 3)]
    zdev = [dev(ahead(z, o), y, c, x) for o in (1, 2, 3)]
    xdev = [dev(z, y, c, ahead(x, o)) for o in (1, 2, 3)]

    def remote(src, dst, ss, rs, to):
        return pltpu.make_async_remote_copy(
            src_ref=src, dst_ref=dst, send_sem=ss, recv_sem=rs, device_id=to, device_id_type=MESH
        )

    loads = [pltpu.make_async_copy(wk, wkv, lsem.at[0])]
    for j in range(4):
        loads.append(
            pltpu.make_async_copy(
                tok.at[pl.ds(j * CHUNK, CHUNK)], tokv.at[pl.ds(j * CHUNK, CHUNK)], lsem.at[1 + j]
            )
        )
        if j == 0:
            loads.append(pltpu.make_async_copy(wv, wvv, lsem.at[5]))
    loads.append(pltpu.make_async_copy(wq, wqv, lsem.at[6]))
    loads.append(pltpu.make_async_copy(wo, wof.at[x], lsem.at[7]))
    for copy in loads:
        copy.start()

    barrier = pltpu.get_barrier_semaphore()
    for to in [partner] + ydev + zdev + xdev:
        pl.semaphore_signal(barrier, inc=1, device_id=to, device_id_type=MESH)

    scale = 128.0**-0.25
    omega = om[...] * (scale * LOG2E)
    om_hi = omega.astype(BF)
    om_lo = (omega - om_hi.astype(F32)).astype(BF)
    omw[pl.ds(0, 128)] = om_hi
    omw[pl.ds(128, 128)] = om_hi
    omw[pl.ds(256, 128)] = om_lo
    omw[pl.ds(384, 128)] = jnp.full((128, 256), -1.0, BF)
    run[...] = jnp.zeros_like(run)

    low = lax.broadcasted_iota(jnp.int32, (CHUNK, 128), 1) < 64

    def features(p):
        hi = p.astype(BF)
        lo = (p - hi.astype(F32)).astype(BF)
        square = p * p * (0.5 * scale * scale * LOG2E)
        pair = square + pltpu.roll(square, 64, 1) + 4.0 / 64
        pair_hi = pair.astype(BF).astype(F32)
        sums = jnp.where(low, pair_hi, pair - pair_hi).astype(BF)
        power = dot(jnp.concatenate([hi, lo, hi, sums], axis=1), omw[...])
        return (jnp.exp2(power) + 0.001 / 16).astype(BF)

    pl.semaphore_wait(barrier, 10)

    half = c * 256
    share = (256 - DIRECT) // 4
    mine = lax.select(c == 0, y, z)
    at_direct = pl.multiple_of(half, 64)
    at_piece = pl.multiple_of(half + DIRECT + mine * share, 16)
    w_direct = [
        remote(wo.at[pl.ds(at_direct, DIRECT)], wof.at[x, pl.ds(at_direct, DIRECT)],
               wsd.at[i], wqd.at[i], xdev[i])
        for i in range(3)
    ]
    w_piece = [
        remote(wo.at[pl.ds(at_piece, share)], wof.at[x, pl.ds(at_piece, share)],
               wsx.at[i], wqx.at[i], xdev[i])
        for i in range(3)
    ]
    for copy in w_piece + w_direct:
        copy.start()

    loads[0].wait()
    loads[2].wait()

    def key_value(j):
        rows = pl.ds(pl.multiple_of(j * CHUNK, CHUNK), CHUNK)
        t = tokv[rows]
        k = dot(t, wkv[...])
        v = dot(t, wvv[...])
        vv[rows] = v.astype(BF)
        for h in range(4):
            feat = features(k[:, h * 128 : (h + 1) * 128])
            kf[rows, h * 256 : (h + 1) * 256] = feat
            turned = jnp.concatenate(
                [v[:, h * 128 : (h + 1) * 128].T.astype(BF), jnp.ones((NORM, CHUNK), BF)], axis=0
            )
            so_far = run[h]
            sloc[j, h] = so_far.astype(BF)
            run[h] = so_far + dot(turned, feat)

    for j in range(4):
        loads[1 if j == 0 else 2 + j].wait()
        key_value(j)

    first, other = 2 * c, 2 - 2 * c
    sx[...] = run[pl.ds(other, 2)].astype(BF)
    round0 = remote(sx, r0, s0, q0, partner)
    round0.start()

    causal = lax.broadcasted_iota(jnp.int32, (CHUNK, CHUNK), 0) >= lax.broadcasted_iota(
        jnp.int32, (CHUNK, CHUNK), 1
    )
    ones = jnp.ones((CHUNK, 128), BF)

    def query(j):
        rows = pl.ds(j * CHUNK, CHUNK)
        q = dot(tokv[rows], wqv[...])
        for h in range(4):
            qf[rows, h * 256 : (h + 1) * 256] = features(q[:, h * 128 : (h + 1) * 128])

    def inside(j):
        rows = pl.ds(j * CHUNK, CHUNK)
        for h in range(4):
            feat = qf[rows, h * 256 : (h + 1) * 256]
            scores = dot_nt(feat, kf[rows, h * 256 : (h + 1) * 256])
            weights = jnp.where(causal, scores, 0.0).astype(BF)
            value = jnp.concatenate([vv[rows, h * 128 : (h + 1) * 128], ones], axis=1)
            total = dot(weights, value)
            if j > 0:
                total = total + dot_nt(feat, widen(sloc[j, h]))
            acc[h, rows] = total

    loads[6].wait()
    query(0)

    round0.wait()
    chip = run[pl.ds(first, 2)] + r0[...].astype(F32)
    ua[...] = chip[:, :, :128]
    pb[...] = jnp.zeros_like(pb)
    ma[...] = chip[:, :, :128].astype(BF)
    mb[...] = chip[:, :, 128:].astype(BF)
    round1a = [remote(ma, ra.at[i], s1a.at[i], q1a.at[i], ydev[i]) for i in range(3)]
    round1b = [remote(mb, rb.at[i], s1b.at[i], q1b.at[i], zdev[i]) for i in range(3)]
    for i in range(3):
        round1a[i].start()
        pl.when(z + i + 1 < 4)(round1b[i].start)

    query(1)
    query(2)
    inside(0)

    pa[...] = jnp.zeros_like(pa)
    for i in range(3):
        round1a[i].wait()
        got = ra[i].astype(F32)
        ua[...] += got
        pa[...] += jnp.where(y >= i + 1, got, 0.0)
        pl.when(z + i + 1 < 4)(round1b[i].wait_send)

        @pl.when(z >= i + 1)
        def _():
            round1b[i].wait_recv()
            pb[...] += rb[i].astype(F32)

    ma2[...] = ua[...].astype(BF)
    mb2[0] = pb[...].astype(BF)
    mb2[1] = (pb[...] + mb[...].astype(F32)).astype(BF)
    round2a = [remote(ma2, ra2.at[i], s2a.at[i], q2a.at[i], zdev[i]) for i in range(3)]
    round2b = [
        remote(mb2.at[lax.select(y + i + 1 < 4, 1, 0)], rb2.at[i], s2b.at[i], q2b.at[i], ydev[i])
        for i in range(3)
    ]
    for i in range(3):
        round2b[i].start()
        pl.when(z + i + 1 < 4)(round2a[i].start)

    query(3)
    inside(1)

    w_on = []
    for i in range(3):
        w_piece[i].wait()
        source = ahead(x, 3 - i)
        for n in range(3):
            to = dev(
                lax.select(c == 0, z, ahead(z, n + 1)), lax.select(c == 0, ahead(y, n + 1), y), c, x
            )
            w_on.append(
                remote(
                    wof.at[source, pl.ds(at_piece, share)], wof.at[source, pl.ds(at_piece, share)],
                    wsy.at[i, n], wqy.at[i, n], to,
                )
            )
    for copy in w_on:
        copy.start()

    inside(2)
    inside(3)

    for i in range(3):
        round2b[i].wait()
        pb[...] += rb2[i].astype(F32)
        pl.when(z + i + 1 < 4)(round2a[i].wait_send)

        @pl.when(z >= i + 1)
        def _():
            round2a[i].wait_recv()
            pa[...] += ra2[i].astype(F32)

    before = jnp.concatenate([pa[...], pb[...]], axis=2)
    here = run[pl.ds(first, 2)]
    ps[...] = jnp.where(c == 0, before + here, before).astype(BF)
    round3 = remote(ps, pf.at[pl.ds(first, 2)], s3, q3, partner)
    round3.start()
    pf[pl.ds(first, 2)] = jnp.where(c == 1, before + r0[...].astype(F32), before).astype(BF)
    round3.wait()

    exchange = []
    for o in (2, 1, 3, 0):
        j = ahead(x, o)
        rows = pl.ds(pl.multiple_of(j * CHUNK, CHUNK), CHUNK)
        for h in range(4):
            feat = qf[rows, h * 256 : (h + 1) * 256]
            total = acc[h, rows] + dot_nt(feat, widen(pf[h]))
            atts[o, :, h * 128 : (h + 1) * 128] = (total[:, :128] / total[:, 128:]).astype(BF)
        if o:
            copy = remote(atts.at[o], attb.at[o - 1], sA.at[o - 1], qA.at[o - 1], xdev[o - 1])
            copy.start()
            exchange.append((o, copy))

    loads[7].wait()

    for copy in w_on + w_direct:
        copy.wait()
    w_pair = []
    for i in range(3):
        rows = pl.ds(pl.multiple_of(half, 256), 256)
        source = ahead(x, 3 - i)
        w_pair.append(
            remote(wof.at[source, rows], wof.at[source, rows], wsp.at[i], wqp.at[i], partner)
        )
        w_pair[i].start()

    res[...] = dot(atts[0], wof[x])
    for i in range(3):
        w_pair[i].wait()
    for o, copy in sorted(exchange, key=lambda pair: -(pair[0] % 2)):
        copy.wait()
        res[...] += dot(attb[o - 1], wof[ahead(x, 4 - o)])
    out[...] = res[...].astype(BF)


def shards(tokens, w_query, w_key, w_value, omega, w_out):
    dma = pltpu.SemaphoreType.DMA
    state = (2, 128 + NORM, 256)
    part = (2, 128 + NORM, 128)
    anywhere = pl.BlockSpec(memory_space=pl.ANY)
    vmem = pl.BlockSpec(memory_space=pltpu.VMEM)
    V = pltpu.VMEM
    return pl.pallas_call(
        kernel,
        out_shape=jax.ShapeDtypeStruct((CHUNK, 2048), BF),
        in_specs=[anywhere, anywhere, anywhere, anywhere, vmem, anywhere],
        out_specs=vmem,
        scratch_shapes=[
            V((1024, 2048), BF), V((2048, 512), BF), V((2048, 512), BF), V((2048, 512), BF),
            V((4, 512, 2048), BF), V((1024, 1024), BF), V((1024, 1024), BF), V((1024, 512), BF),
            V((512, 256), BF), V((4, 128 + NORM, 256), F32), V((4, 4, 128 + NORM, 256), BF),
            V((4, 1024, 256), F32), V((CHUNK, 2048), F32),
            V(state, BF), V(state, BF),
            V(part, BF), V((3,) + part, BF), V(part, BF), V((3,) + part, BF),
            V(part, BF), V((3,) + part, BF), V((2,) + part, BF), V((3,) + part, BF),
            V(part, F32), V(part, F32), V(part, F32),
            V(state, BF), V((4, 128 + NORM, 256), BF),
            V((4, CHUNK, 512), BF), V((3, CHUNK, 512), BF),
            dma((8,)), dma(()), dma(()),
            dma((3,)), dma((3,)), dma((3,)), dma((3,)), dma((3,)), dma((3,)), dma((3,)), dma((3,)),
            dma(()), dma(()), dma((3,)), dma((3,)),
            dma((3,)), dma((3,)), dma((3,)), dma((3,)), dma((3, 3)), dma((3, 3)), dma((3,)), dma((3,)),
        ],
        compiler_params=pltpu.CompilerParams(
            collective_id=0, has_side_effects=True, vmem_limit_bytes=60 << 20
        ),
        name="causal_linear",
    )(tokens, w_query, w_key, w_value, omega, w_out)


def solution(mesh):
    placed = (
        P("seq", None), P(None, "head"), P(None, "head"), P(None, "head"), P(), P("head", None),
    )
    return jax.shard_map(
        shards, mesh=mesh, in_specs=placed, out_specs=P(("seq", "head"), None), check_vma=False
    )
```

time: 243 us -> 54.2 us (0.22)
  waiting for transfers between devices: 110 us -> 0 us
  Pallas kernels: 0 us -> 51.7 us
  other arithmetic: 43.2 us -> 0 us
  matrix products: 40.1 us -> 0 us
  blocking collectives: 27.5 us -> 0 us
  between operations: 13.8 us -> 0.01 us
  local copies, waits for them, and re-layouts: 5.4 us -> 2.3 us
    reduce_scatter x1 -> x0, waiting for transfers between devices: 79.6 us -> none  [shards(): lax.psum_scatter(jnp.dot(attention, w_out, preferred_element_type=jnp.flo...]
    pallas_call x0 -> x1, Pallas kernels: none -> 51.7 us  [shards(): pl.pallas_call(kernel, out_shape=jax.ShapeDtypeStruct((CHUNK, 2048), BF),...]
    dot_general x16 -> x0, matrix products: 40.1 us -> none  [the longest x2 9.57 us: feature_map(): jnp.einsum('thd,dm->thm', scaled, omega, precision=highest_precision)]
    select_n x62 -> x0, other arithmetic: 38.3 us -> none  [turn(): jnp.where(position < mine, new, old)]
    all_gather x1 -> x0, waiting for transfers between devices: 30.8 us -> none  [prefix(): pieces = jax.tree.map(lambda part: lax.all_gather(part, axis), value)]
    all_gather x1 -> x0, blocking collectives: 27.5 us -> none  [prefix(): pieces = jax.tree.map(lambda part: lax.all_gather(part, axis), value)]
    unnamed x36 -> x1, local copies, waits for them, and re-layouts: 5.32 us -> 2.3 us
    convert_element_type x1 -> x0, other arithmetic: 2.71 us -> none  [shards(): return mixed.astype(jnp.bfloat16)]
  transfers between devices with their start and end apart: 2 -> 0, of which waited for: 2 -> 0; matrix products, arithmetic and copies ran while one was open for 6% -> 0% of each run, Pallas kernels for 0% -> 0%
where the time goes in v1:
time: 54.2 us; the launch traced here: 54 us
  Pallas kernels  51.7 us (95%)
  local copies, waits for them, and re-layouts  2.3 us (4%)
    pallas_call x1, Pallas kernels, shards(): pl.pallas_call(kernel, out_shape=jax.ShapeDtypeStruct((CHUNK, 2048), BF),...  51.7 us
    unnamed x1, local copies, waits for them, and re-layouts  2.3 us

profile of v1, /device:TPU:1, one launch (start us, length us, event | category | flops | bytes accessed | tf_op | source)
XLA Modules:
  0.0 54.0 jit_solution(10335708620375229922)
XLA Ops:
  0.0 51.7 %causal_linear.1 = bf16[256,2048]{1,0:T(8,128)(2,1)} custom-call(bf16[1024,2048]{1,0:T(8,128)(2,1)} %tok.1, bf16[2048,512]{1,0:T(8,128)(2,1)} %wq.1, bf16[2048,512]{1,0:T(8,128)(2,1)} %wk.1, bf16[2048,512]{1,0:T(8,128)(2,1)} %wv.1, f32[128,256]{1,0:T(8,128)} %om.1, bf16[512,2048]{1,0:T(8,128)(2,1)} %wo.1), custom_call_target="tpu_custom_call" | custom-call | tf_op jit(solution)/shard_map/causal_linear/pallas_call | solution.py:297
  51.7 2.3 %copy.8 = bf16[256,2048]{1,0:T(8,128)(2,1)} copy(bf16[256,2048]{1,0:T(8,128)(2,1)} %causal_linear.1) | data formatting | bytes 2097152

commit v2 on v1

v2 whole, which is shorter than its diff:
```python
import jax
import jax.numpy as jnp
from jax import lax
from jax.experimental import pallas as pl
from jax.experimental.pallas import tpu as pltpu
from jax.sharding import PartitionSpec as P

MESH = pl.DeviceIdType.MESH
BF, F32 = jnp.bfloat16, jnp.float32
LOG2E = 1.4426950408889634
CHUNK = 256
GROUPS = 2
NH = 4 // GROUPS
PIECE = 64

NT = (((1,), (1,)), ((), ()))


def dot(a, b):
    return jnp.dot(a, b, preferred_element_type=F32)


def dot_nt(a, b):
    return lax.dot_general(a, b, NT, preferred_element_type=F32)


def kernel(
    tok, wq, wk, wv, om, wo, out,
    tokv, wqv, wkv, omv, wof, kf, qf, vv, omw, run, sloc, acc, res,
    r0, ma, ra, ma2, ra2, mb, rb, mb2, rb2, pa, ua, pb, ps, pf, pw, atts, attb,
    lsem, s0, q0, s1a, q1a, s1b, q1b, s2a, q2a, s2b, q2b, s3, q3, sA, qA,
    wsx, wqx, wsy, wqy, wsz, wqz, wsp, wqp,
):
    seq, x = lax.axis_index("seq"), lax.axis_index("head")
    z, y, c = lax.div(seq, 8), lax.rem(lax.div(seq, 2), 4), lax.rem(seq, 2)

    def ahead(v, o):
        return lax.rem(v + o, 4)

    def dev(z_, y_, c_, x_):
        return {"seq": z_ * 8 + y_ * 2 + c_, "head": x_}

    partner = dev(z, y, 1 - c, x)
    ydev = [dev(z, ahead(y, o), c, x) for o in (1, 2, 3)]
    zdev = [dev(ahead(z, o), y, c, x) for o in (1, 2, 3)]
    xdev = [dev(z, y, c, ahead(x, o)) for o in (1, 2, 3)]

    def remote(src, dst, ss, rs, to):
        return pltpu.make_async_remote_copy(
            src_ref=src, dst_ref=dst, send_sem=ss, recv_sem=rs, device_id=to, device_id_type=MESH
        )

    def load(src, dst, i):
        copy = pltpu.make_async_copy(src, dst, lsem.at[i])
        copy.start()
        return copy

    def rows_of(j):
        return pl.ds(j * CHUNK, CHUNK)

    load_om = load(om, omv, 0)
    load_tok, load_kv = [], []
    for j in range(4):
        load_tok.append(load(tok.at[rows_of(j)], tokv.at[rows_of(j)], 1 + j))
        if j == 0:
            for g in range(GROUPS):
                cols = pl.ds(g * NH * 128, NH * 128)
                load_kv.append(
                    (
                        load(wk.at[:, cols], wkv.at[g, :, pl.ds(0, NH * 128)], 5 + 2 * g),
                        load(wv.at[:, cols], wkv.at[g, :, pl.ds(NH * 128, NH * 128)], 6 + 2 * g),
                    )
                )
    load_q = load(wq, wqv, 13)
    load_o = load(wo, wof.at[x], 14)

    barrier = pltpu.get_barrier_semaphore()
    for to in [partner] + ydev + zdev + xdev:
        pl.semaphore_signal(barrier, inc=1, device_id=to, device_id_type=MESH)

    run[...] = jnp.zeros_like(run)
    load_om.wait()

    scale = 128.0**-0.25
    omega = omv[...] * (scale * LOG2E)
    om_hi = omega.astype(BF)
    om_lo = (omega - om_hi.astype(F32)).astype(BF)
    omw[pl.ds(0, 128)] = om_hi
    omw[pl.ds(128, 128)] = om_hi
    omw[pl.ds(256, 128)] = om_lo
    omw[pl.ds(384, 128)] = jnp.full((128, 256), -1.0, BF)

    low = lax.broadcasted_iota(jnp.int32, (CHUNK, 128), 1) < 64

    def features(p):
        hi = p.astype(BF)
        lo = (p - hi.astype(F32)).astype(BF)
        square = p * p * (0.5 * scale * scale * LOG2E)
        pair = square + pltpu.roll(square, 64, 1) + 4.0 / 64
        pair_hi = pair.astype(BF).astype(F32)
        sums = jnp.where(low, pair_hi, pair - pair_hi).astype(BF)
        power = dot(jnp.concatenate([hi, lo, hi, sums], axis=1), omw[...])
        return (jnp.exp2(power) + 0.001 / 16).astype(BF)

    pl.semaphore_wait(barrier, 10)

    half = c * 256
    mine = lax.select(c == 0, y, z)

    def piece(o, start=0, size=PIECE):
        return pl.ds(pl.multiple_of(half + ahead(mine, o) * PIECE + start, 32), size)

    def along(o):
        return dev(
            lax.select(c == 0, z, ahead(z, o)), lax.select(c == 0, ahead(y, o), y), c, x
        )

    ends = [along(1), along(3)]
    w_x, w_y, w_z, w_p = [], [], [], []
    for i in range(3):
        source = ahead(x, 3 - i)
        shard = wof.at[source]
        w_x.append(
            remote(wo.at[piece(0)], wof.at[x, piece(0)], wsx.at[i], wqx.at[i], xdev[i])
        )
        w_y.append(
            [remote(shard.at[piece(0)], shard.at[piece(0)], wsy.at[i, d], wqy.at[i, d], ends[d])
             for d in range(2)]
        )
        spans = [piece(3, 0, 32), piece(1, 32, 32)]
        w_z.append(
            [remote(shard.at[spans[d]], shard.at[spans[d]], wsz.at[i, d], wqz.at[i, d], ends[d])
             for d in range(2)]
        )
        spans = [piece(0), piece(3), piece(1), piece(2, 0, 32), piece(2, 32, 32)]
        w_p.append(
            [remote(shard.at[span], shard.at[span], wsp.at[i, n], wqp.at[i, n], partner)
             for n, span in enumerate(spans)]
        )
    for i in range(3):
        w_x[i].start()

    def w_first(i):
        w_x[i].wait_recv()
        w_y[i][0].start()
        w_y[i][1].start()
        w_p[i][0].start()

    def w_second(i):
        for d in range(2):
            w_y[i][d].wait_recv()
            w_z[i][d].start()
            w_p[i][1 + d].start()

    def w_third(i):
        for d in range(2):
            w_z[i][d].wait_recv()
            w_p[i][3 + d].start()

    def key_value(g, j):
        rows = rows_of(j)
        both = dot(tokv[rows], wkv[g])
        for i in range(NH):
            h = g * NH + i
            feat = features(both[:, i * 128 : (i + 1) * 128])
            v = both[:, (NH + i) * 128 : (NH + i + 1) * 128]
            kf[rows, h * 256 : (h + 1) * 256] = feat
            vv[rows, h * 128 : (h + 1) * 128] = v.astype(BF)
            turned = v.T.astype(BF)
            norm = jnp.ones((16, CHUNK), BF)
            state = dot(jnp.concatenate([turned[:64], norm, turned[64:], norm], axis=0), feat)
            for a in range(2):
                for l in range(2):
                    so_far = run[l, h, a]
                    sloc[j, h, a * 80 : a * 80 + 80, l * 128 : (l + 1) * 128] = so_far.astype(BF)
                    run[l, h, a] = so_far + state[a * 80 : a * 80 + 80, l * 128 : (l + 1) * 128]

    causal = lax.broadcasted_iota(jnp.int32, (CHUNK, CHUNK), 0) >= lax.broadcasted_iota(
        jnp.int32, (CHUNK, CHUNK), 1
    )
    ones = jnp.ones((CHUNK, 128), BF)

    def query(j):
        rows = rows_of(j)
        q = dot(tokv[rows], wqv[...])
        for h in range(4):
            qf[rows, h * 256 : (h + 1) * 256] = features(q[:, h * 128 : (h + 1) * 128])

    def inside(g, j):
        rows = rows_of(j)
        for h in range(g * NH, (g + 1) * NH):
            feat = qf[rows, h * 256 : (h + 1) * 256]
            scores = dot_nt(feat, kf[rows, h * 256 : (h + 1) * 256])
            weights = jnp.where(causal, scores, 0.0).astype(BF)
            value = jnp.concatenate([vv[rows, h * 128 : (h + 1) * 128], ones], axis=1)
            total = dot(weights, value)
            if j > 0:
                local = sloc[j, h]
                norm = local[64:80]
                total = total + dot_nt(
                    feat, jnp.concatenate([local[:64], local[80:144]] + [norm] * 8, axis=0)
                )
            acc[h, rows] = total

    def heads(g):
        return pl.ds(g * NH, NH)

    def round0(g):
        return remote(run.at[1 - c, heads(g)], r0.at[heads(g)], s0.at[g], q0.at[g], partner)

    def round1(g):
        return (
            [remote(ma.at[heads(g)], ra.at[i, heads(g)], s1a.at[g, i], q1a.at[g, i], ydev[i]) for i in range(3)],
            [remote(mb.at[heads(g)], rb.at[i, heads(g)], s1b.at[g, i], q1b.at[g, i], zdev[i]) for i in range(3)],
        )

    def round2(g):
        return (
            [remote(ma2.at[heads(g)], ra2.at[i, heads(g)], s2a.at[g, i], q2a.at[g, i], zdev[i]) for i in range(3)],
            [
                remote(
                    mb2.at[lax.select(y + i + 1 < 4, 1, 0), heads(g)], rb2.at[i, heads(g)],
                    s2b.at[g, i], q2b.at[g, i], ydev[i],
                )
                for i in range(3)
            ],
        )

    def round3(g):
        return remote(ps.at[heads(g)], pf.at[c, heads(g)], s3.at[g], q3.at[g], partner)

    def start1(g):
        hs = heads(g)
        round0(g).wait()
        chip = run[c, hs] + r0[hs]
        ua[hs] = chip[:, 0]
        ma[hs] = chip[:, 0].astype(BF)
        mb[hs] = chip[:, 1].astype(BF)
        over_y, over_z = round1(g)
        for i in range(3):
            over_y[i].start()
            pl.when(z + i + 1 < 4)(over_z[i].start)

    def start2(g):
        hs = heads(g)
        over_y, over_z = round1(g)
        pa[hs] = jnp.zeros((NH, 80, 128), F32)
        pb[hs] = jnp.zeros((NH, 80, 128), F32)
        for i in range(3):
            over_y[i].wait()
            got = ra[i, hs].astype(F32)
            ua[hs] += got
            pa[hs] += jnp.where(y >= i + 1, got, 0.0)
            pl.when(z + i + 1 < 4)(over_z[i].wait_send)

            @pl.when(z >= i + 1)
            def _():
                over_z[i].wait_recv()
                pb[hs] += rb[i, hs].astype(F32)

        ma2[hs] = ua[hs].astype(BF)
        mb2[0, hs] = pb[hs].astype(BF)
        mb2[1, hs] = (pb[hs] + mb[hs].astype(F32)).astype(BF)
        over_z, over_y = round2(g)
        for i in range(3):
            over_y[i].start()
            pl.when(z + i + 1 < 4)(over_z[i].start)

    def start3(g):
        hs = heads(g)
        over_z, over_y = round2(g)
        for i in range(3):
            over_y[i].wait()
            pb[hs] += rb2[i, hs].astype(F32)
            pl.when(z + i + 1 < 4)(over_z[i].wait_send)

            @pl.when(z >= i + 1)
            def _():
                over_z[i].wait_recv()
                pa[hs] += ra2[i, hs].astype(F32)

        for a, part in enumerate((pa, pb)):
            before = part[hs]
            ps[hs, a] = jnp.where(c == 0, before + run[c, hs, a], before).astype(BF)
            pf[c, hs, a] = jnp.where(c == 1, before + r0[hs, a], before).astype(BF)
        round3(g).start()

    def exchange(g, o):
        return remote(atts.at[o, g], attb.at[o - 1, g], sA.at[g, o - 1], qA.at[g, o - 1], xdev[o - 1])

    def combine(g):
        round3(g).wait()
        for h in range(g * NH, (g + 1) * NH):
            for l in range(2):
                norm = pf[l, h, 0, 64:80]
                pw[h, :, l * 128 : (l + 1) * 128] = jnp.concatenate(
                    [pf[l, h, 0, 0:64], pf[l, h, 1, 0:64]] + [norm] * 8, axis=0
                )
        for o in (2, 1, 3, 0):
            rows = pl.ds(pl.multiple_of(ahead(x, o) * CHUNK, CHUNK), CHUNK)
            for i in range(NH):
                h = g * NH + i
                total = acc[h, rows] + dot_nt(qf[rows, h * 256 : (h + 1) * 256], pw[h])
                atts[o, g, :, i * 128 : (i + 1) * 128] = (total[:, :128] / total[:, 128:]).astype(BF)
            if o:
                exchange(g, o).start()

    def project(g, o):
        source = ahead(x, 4 - o) if o else x
        att = attb[o - 1, g] if o else atts[0, g]
        return dot(att, wof[source, pl.ds(g * NH * 128, NH * 128)])

    for copy in load_kv[0]:
        copy.wait()
    for j in range(4):
        load_tok[j].wait()
        key_value(0, j)
    round0(0).start()
    for copy in load_kv[1]:
        copy.wait()
    key_value(1, 0)
    key_value(1, 1)
    start1(0)
    key_value(1, 2)
    key_value(1, 3)
    round0(1).start()
    load_q.wait()
    query(0)
    start1(1)
    w_first(0)
    w_first(2)
    query(1)
    start2(0)
    query(2)
    query(3)
    w_first(1)
    for j in range(4):
        inside(0, j)
    start2(1)
    w_second(0)
    w_second(2)
    start3(0)
    for j in range(4):
        inside(1, j)
    combine(0)
    load_o.wait()
    res[...] = project(0, 0)
    w_second(1)
    w_third(0)
    w_third(2)
    start3(1)
    combine(1)
    w_third(1)
    res[...] += project(1, 0)
    for i in (0, 2, 1):
        for copy in w_p[i]:
            copy.wait_recv()
        exchange(0, i + 1).wait()
        res[...] += project(0, i + 1)
    for i in (0, 2):
        exchange(1, i + 1).wait()
        res[...] += project(1, i + 1)
    exchange(1, 2).wait()
    out[...] = (res[...] + project(1, 2)).astype(BF)
    for i in range(3):
        for copy in [w_x[i]] + w_y[i] + w_z[i] + w_p[i]:
            copy.wait_send()


def shards(tokens, w_query, w_key, w_value, omega, w_out):
    dma = pltpu.SemaphoreType.DMA
    V = pltpu.VMEM
    part = (4, 80, 128)
    whole = (4, 2, 80, 128)
    return pl.pallas_call(
        kernel,
        out_shape=jax.ShapeDtypeStruct((CHUNK, 2048), BF),
        in_specs=[pl.BlockSpec(memory_space=pltpu.HBM)] * 6,
        out_specs=pl.BlockSpec(memory_space=pltpu.VMEM),
        scratch_shapes=[
            V((1024, 2048), BF), V((2048, 512), BF), V((GROUPS, 2048, NH * 256), BF), V((128, 256), F32),
            V((4, 512, 2048), BF), V((1024, 1024), BF), V((1024, 1024), BF), V((1024, 512), BF),
            V((512, 256), BF), V((2,) + whole, F32), V((4, 4, 160, 256), BF),
            V((4, 1024, 256), F32), V((CHUNK, 2048), F32),
            V(whole, F32), V(part, BF), V((3,) + part, BF), V(part, BF), V((3,) + part, BF),
            V(part, BF), V((3,) + part, BF), V((2,) + part, BF), V((3,) + part, BF),
            V(part, F32), V(part, F32), V(part, F32),
            V(whole, BF), V((2,) + whole, BF), V((4, 256, 256), BF),
            V((4, GROUPS, CHUNK, NH * 128), BF), V((3, GROUPS, CHUNK, NH * 128), BF),
            dma((15,)), dma((GROUPS,)), dma((GROUPS,)),
            dma((GROUPS, 3)), dma((GROUPS, 3)), dma((GROUPS, 3)), dma((GROUPS, 3)),
            dma((GROUPS, 3)), dma((GROUPS, 3)), dma((GROUPS, 3)), dma((GROUPS, 3)),
            dma((GROUPS,)), dma((GROUPS,)), dma((GROUPS, 3)), dma((GROUPS, 3)),
            dma((3,)), dma((3,)), dma((3, 2)), dma((3, 2)), dma((3, 2)), dma((3, 2)), dma((3, 5)), dma((3, 5)),
        ],
        compiler_params=pltpu.CompilerParams(
            collective_id=0, has_side_effects=True, vmem_limit_bytes=42 << 20
        ),
        name="causal_linear",
    )(*[pltpu.with_memory_space_constraint(a, pltpu.HBM) for a in (tokens, w_query, w_key, w_value, omega, w_out)])


def solution(mesh):
    placed = (
        P("seq", None), P(None, "head"), P(None, "head"), P(None, "head"), P(), P("head", None),
    )
    return jax.shard_map(
        shards, mesh=mesh, in_specs=placed, out_specs=P(("seq", "head"), None), check_vma=False
    )
```

time: 54.2 us -> 52.8 us (0.974)
  local copies, waits for them, and re-layouts: 2.3 us -> 0.97 us
    unnamed x1, local copies, waits for them, and re-layouts: 2.3 us -> 0.97 us
where the time goes in v2:
time: 52.8 us; the launch traced here: 52.7 us
  Pallas kernels  51.7 us (98%)
  local copies, waits for them, and re-layouts  0.97 us (2%)
    pallas_call x1, Pallas kernels, shards(): pl.pallas_call(kernel, out_shape=jax.ShapeDtypeStruct((CHUNK, 2048), BF),...  51.7 us

profile of v2, /device:TPU:1, one launch (start us, length us, event | category | flops | bytes accessed | tf_op | source)
XLA Modules:
  0.0 52.7 jit_solution(8204492742435244309)
XLA Ops:
  0.0 51.7 %causal_linear.1 = bf16[256,2048]{1,0:T(8,128)(2,1)S(1)} custom-call(bf16[1024,2048]{1,0:T(8,128)(2,1)} %tok.1, bf16[2048,512]{1,0:T(8,128)(2,1)} %wq.1, bf16[2048,512]{1,0:T(8,128)(2,1)} %wk.1, bf16[2048,512]{1,0:T(8,128)(2,1)} %wv.1, f32[128,256]{1,0:T(8,128)} %om.1, bf16[512,2048]{1,0:T(8,128)(2,1)} %wo.1), custom_call_target="tpu_custom_call" | custom-call | tf_op jit(solution)/shard_map/causal_linear/pallas_call | solution.py:375
  51.7 1.0 %copy.8 = bf16[256,2048]{1,0:T(8,128)(2,1)} copy(bf16[256,2048]{1,0:T(8,128)(2,1)S(1)} %causal_linear.1) | data formatting | bytes 2097152

commit v3 on v2

--- a/solution.py
+++ b/solution.py
@@ -9,9 +9,11 @@
 BF, F32 = jnp.bfloat16, jnp.float32
 LOG2E = 1.4426950408889634
 CHUNK = 256
-GROUPS = 2
+GROUPS = 4
 NH = 4 // GROUPS
-PIECE = 64
+DIRECT = 64
+PIECE = (256 - DIRECT) // 4
+HALF = (16, PIECE - 16) if PIECE % 32 else (PIECE // 2, PIECE // 2)
 
 NT = (((1,), (1,)), ((), ()))
 
@@ -29,7 +31,7 @@
     tokv, wqv, wkv, omv, wof, kf, qf, vv, omw, run, sloc, acc, res,
     r0, ma, ra, ma2, ra2, mb, rb, mb2, rb2, pa, ua, pb, ps, pf, pw, atts, attb,
     lsem, s0, q0, s1a, q1a, s1b, q1b, s2a, q2a, s2b, q2b, s3, q3, sA, qA,
-    wsx, wqx, wsy, wqy, wsz, wqz, wsp, wqp,
+    wss, wqs, wsp, wqp,
 ):
     seq, x = lax.axis_index("seq"), lax.axis_index("head")
     z, y, c = lax.div(seq, 8), lax.rem(lax.div(seq, 2), 4), lax.rem(seq, 2)
@@ -60,25 +62,29 @@
 
     load_om = load(om, omv, 0)
     load_tok, load_kv = [], []
+    def load_group(g):
+        cols = pl.ds(g * NH * 128, NH * 128)
+        load_kv.append(
+            (
+                load(wk.at[:, cols], wkv.at[g, :, pl.ds(0, NH * 128)], 5 + 2 * g),
+                load(wv.at[:, cols], wkv.at[g, :, pl.ds(NH * 128, NH * 128)], 6 + 2 * g),
+            )
+        )
+
     for j in range(4):
         load_tok.append(load(tok.at[rows_of(j)], tokv.at[rows_of(j)], 1 + j))
         if j == 0:
-            for g in range(GROUPS):
-                cols = pl.ds(g * NH * 128, NH * 128)
-                load_kv.append(
-                    (
-                        load(wk.at[:, cols], wkv.at[g, :, pl.ds(0, NH * 128)], 5 + 2 * g),
-                        load(wv.at[:, cols], wkv.at[g, :, pl.ds(NH * 128, NH * 128)], 6 + 2 * g),
-                    )
-                )
-    load_q = load(wq, wqv, 13)
-    load_o = load(wo, wof.at[x], 14)
+            load_group(0)
+    load_q = []
 
     barrier = pltpu.get_barrier_semaphore()
     for to in [partner] + ydev + zdev + xdev:
         pl.semaphore_signal(barrier, inc=1, device_id=to, device_id_type=MESH)
 
     run[...] = jnp.zeros_like(run)
+    for copy in [load_tok[0], *load_kv[0]]:
+        copy.wait()
+    held = [dot(tokv[rows_of(0)], wkv[0])]
     load_om.wait()
 
     scale = 128.0**-0.25
@@ -108,43 +114,57 @@
     mine = lax.select(c == 0, y, z)
 
     def piece(o, start=0, size=PIECE):
-        return pl.ds(pl.multiple_of(half + ahead(mine, o) * PIECE + start, 32), size)
+        return pl.ds(pl.multiple_of(half + DIRECT + ahead(mine, o) * PIECE + start, 16), size)
 
     def along(o):
         return dev(
             lax.select(c == 0, z, ahead(z, o)), lax.select(c == 0, ahead(y, o), y), c, x
         )
 
-    ends = [along(1), along(3)]
-    w_x, w_y, w_z, w_p = [], [], [], []
-    for i in range(3):
-        source = ahead(x, 3 - i)
-        shard = wof.at[source]
-        w_x.append(
-            remote(wo.at[piece(0)], wof.at[x, piece(0)], wsx.at[i], wqx.at[i], xdev[i])
-        )
-        w_y.append(
-            [remote(shard.at[piece(0)], shard.at[piece(0)], wsy.at[i, d], wqy.at[i, d], ends[d])
-             for d in range(2)]
-        )
-        spans = [piece(3, 0, 32), piece(1, 32, 32)]
-        w_z.append(
-            [remote(shard.at[spans[d]], shard.at[spans[d]], wsz.at[i, d], wqz.at[i, d], ends[d])
-             for d in range(2)]
-        )
-        spans = [piece(0), piece(3), piece(1), piece(2, 0, 32), piece(2, 32, 32)]
-        w_p.append(
-            [remote(shard.at[span], shard.at[span], wsp.at[i, n], wqp.at[i, n], partner)
-             for n, span in enumerate(spans)]
-        )
-    for i in range(3):
-        w_x[i].start()
+    ends, sides = [along(1), along(3)], [xdev[0], xdev[2]]
+    shard = [wof.at[ahead(x, o)] for o in (3, 1, 2)]
+    direct = pl.ds(pl.multiple_of(half, 64), DIRECT)
+    direct_parts = [pl.ds(pl.multiple_of(half + d * 32, 32), 32) for d in range(2)]
+    piece_parts = [(0, HALF[0]), (HALF[0], HALF[1])]
+
+    def passes(k, i, d, span, to, from_wo=False):
+        where = wof.at[x, span] if from_wo else shard[i].at[span]
+        return remote(wo.at[span] if from_wo else where, where, wss.at[k, i, d], wqs.at[k, i, d], to)
+
+    w_x1 = [passes(0, 0, d, piece(0), sides[d], True) for d in range(2)]
+    w_d1 = [passes(0, 1, d, direct, sides[d], True) for d in range(2)]
+    w_x2 = [passes(1, d, 0, piece(0, *piece_parts[d]), sides[d]) for d in range(2)]
+    w_d2 = [passes(1, d, 1, direct_parts[d], sides[d]) for d in range(2)]
+    w_y = [[passes(2, i, d, piece(0), ends[d]) for d in range(2)] for i in range(3)]
+    w_z = [[passes(3, i, d, piece(3 - 2 * d, *piece_parts[d]), ends[d]) for d in range(2)] for i in range(3)]
+    w_p = [
+        [
+            remote(shard[i].at[span], shard[i].at[span], wsp.at[i, n], wqp.at[i, n], partner)
+            for n, span in enumerate(
+                [piece(0), piece(3), piece(1), piece(2, *piece_parts[0]), piece(2, *piece_parts[1]), direct]
+            )
+        ]
+        for i in range(3)
+    ]
+    for copy in w_x1 + w_d1:
+        copy.start()
+    for g in range(1, GROUPS):
+        load_group(g)
+
+    def w_along_head(i):
+        w_x1[i].wait_recv()
+        w_x2[i].start()
+
+    def w_along_head_direct(i):
+        w_d1[i].wait_recv()
+        w_d2[i].start()
 
     def w_first(i):
-        w_x[i].wait_recv()
+        if i == 2:
+            for copy in w_x2:
+                copy.wait_recv()
         w_y[i][0].start()
         w_y[i][1].start()
-        w_p[i][0].start()
 
     def w_second(i):
         for d in range(2):
@@ -157,9 +177,8 @@
             w_z[i][d].wait_recv()
             w_p[i][3 + d].start()
 
-    def key_value(g, j):
+    def key_value(g, j, both):
         rows = rows_of(j)
-        both = dot(tokv[rows], wkv[g])
         for i in range(NH):
             h = g * NH + i
             feat = features(both[:, i * 128 : (i + 1) * 128])
@@ -180,11 +199,11 @@
     )
     ones = jnp.ones((CHUNK, 128), BF)
 
-    def query(j):
+    def query(n, j, q):
         rows = rows_of(j)
-        q = dot(tokv[rows], wqv[...])
-        for h in range(4):
-            qf[rows, h * 256 : (h + 1) * 256] = features(q[:, h * 128 : (h + 1) * 128])
+        for i in range(2):
+            h = n * 2 + i
+            qf[rows, h * 256 : (h + 1) * 256] = features(q[:, i * 128 : (i + 1) * 128])
 
     def inside(g, j):
         rows = rows_of(j)
@@ -286,7 +305,7 @@
         round3(g).start()
 
     def exchange(g, o):
-        return remote(atts.at[o, g], attb.at[o - 1, g], sA.at[g, o - 1], qA.at[g, o - 1], xdev[o - 1])
+        return remote(atts.at[o, :, pl.ds(g * NH * 128, NH * 128)], attb.at[o - 1, :, pl.ds(g * NH * 128, NH * 128)], sA.at[g, o - 1], qA.at[g, o - 1], xdev[o - 1])
 
     def combine(g):
         round3(g).wait()
@@ -296,75 +315,123 @@
                 pw[h, :, l * 128 : (l + 1) * 128] = jnp.concatenate(
                     [pf[l, h, 0, 0:64], pf[l, h, 1, 0:64]] + [norm] * 8, axis=0
                 )
-        for o in (2, 1, 3, 0):
+        order = (2, 1, 3, 0)
+        totals = []
+        for o in order:
             rows = pl.ds(pl.multiple_of(ahead(x, o) * CHUNK, CHUNK), CHUNK)
-            for i in range(NH):
-                h = g * NH + i
-                total = acc[h, rows] + dot_nt(qf[rows, h * 256 : (h + 1) * 256], pw[h])
-                atts[o, g, :, i * 128 : (i + 1) * 128] = (total[:, :128] / total[:, 128:]).astype(BF)
-            if o:
-                exchange(g, o).start()
-
-    def project(g, o):
+            for h in range(g * NH, (g + 1) * NH):
+                totals.append(acc[h, rows] + dot_nt(qf[rows, h * 256 : (h + 1) * 256], pw[h]))
+        for o in order:
+            for h in range(g * NH, (g + 1) * NH):
+                total = totals.pop(0)
+                atts[o, :, h * 128 : (h + 1) * 128] = (total[:, :128] / total[:, 128:]).astype(BF)
+        for o in order[:3]:
+            exchange(g, o).start()
+
+    def project(o, start, stop):
         source = ahead(x, 4 - o) if o else x
-        att = attb[o - 1, g] if o else atts[0, g]
-        return dot(att, wof[source, pl.ds(g * NH * 128, NH * 128)])
-
-    for copy in load_kv[0]:
+        att = attb[o - 1, :, start:stop] if o else atts[0, :, start:stop]
+        return dot(att, wof[source, start:stop])
+
+    stages = [("kv", g, j) for g in range(GROUPS) for j in range(4)]
+    stages += [("q", n, j) for n in range(2) for j in range(4)]
+
+    def front(kind, g, j):
+        return dot(tokv[rows_of(j)], wqv[g] if kind == "q" else wkv[g])
+
+    def step(count=1):
+        for _ in range(count):
+            (kind, g, j), wide = stages.pop(0), held.pop(0)
+            if stages:
+                held.append(front(*stages[0]))
+            (query if kind == "q" else key_value)(g, j, wide)
+
+    def insides(g):
+        for j in range(4):
+            inside(g, j)
+
+    for copy in load_tok[1:3]:
         copy.wait()
-    for j in range(4):
-        load_tok[j].wait()
-        key_value(0, j)
+    step(2)
+    for copy in [load_tok[3], *load_kv[1]]:
+        copy.wait()
+    step(2)
     round0(0).start()
-    for copy in load_kv[1]:
-        copy.wait()
-    key_value(1, 0)
-    key_value(1, 1)
+    for n in range(2):
+        load_q.append(load(wq.at[:, pl.ds(n * 256, 256)], wqv.at[n], 13 + n))
+    load_o = load(wo, wof.at[x], 15)
+    for g in range(2, GROUPS):
+        for copy in load_kv[g]:
+            copy.wait()
+    step(2)
     start1(0)
-    key_value(1, 2)
-    key_value(1, 3)
+    step(2)
     round0(1).start()
-    load_q.wait()
-    query(0)
+    step(2)
     start1(1)
-    w_first(0)
+    step(2)
+    round0(2).start()
+    w_along_head(0)
+    w_along_head(1)
+    step(2)
+    start2(0)
+    start1(2)
+    load_q[0].wait()
+    load_q[1].wait()
+    step(2)
+    round0(3).start()
+    step(2)
+    start2(1)
+    start1(3)
+    step(2)
+    start3(0)
+    insides(0)
+    start2(2)
+    w_along_head_direct(0)
+    w_along_head_direct(1)
+    combine(0)
+    for i in range(2):
+        w_first(i)
+        w_p[i][0].start()
+        w_p[i][5].start()
+    insides(1)
+    start3(1)
+    start2(3)
     w_first(2)
-    query(1)
-    start2(0)
-    query(2)
-    query(3)
-    w_first(1)
-    for j in range(4):
-        inside(0, j)
-    start2(1)
+    step(2)
+    combine(1)
+    step(2)
+    w_p[2][0].start()
+    insides(2)
+    start3(2)
+    insides(3)
     w_second(0)
+    w_second(1)
+    combine(2)
+    start3(3)
+    load_o.wait()
+    res[...] = project(0, 0, 256)
+    combine(3)
     w_second(2)
-    start3(0)
-    for j in range(4):
-        inside(1, j)
-    combine(0)
-    load_o.wait()
-    res[...] = project(0, 0)
-    w_second(1)
+    for copy in w_d2:
+        copy.wait_recv()
+    w_p[2][5].start()
     w_third(0)
-    w_third(2)
-    start3(1)
-    combine(1)
     w_third(1)
-    res[...] += project(1, 0)
-    for i in (0, 2, 1):
+    res[...] += project(0, 256, 512)
+    for i in range(3):
+        o = (1, 3, 2)[i]
+        if i == 0:
+            w_third(2)
         for copy in w_p[i]:
             copy.wait_recv()
-        exchange(0, i + 1).wait()
-        res[...] += project(0, i + 1)
-    for i in (0, 2):
-        exchange(1, i + 1).wait()
-        res[...] += project(1, i + 1)
-    exchange(1, 2).wait()
-    out[...] = (res[...] + project(1, 2)).astype(BF)
-    for i in range(3):
-        for copy in [w_x[i]] + w_y[i] + w_z[i] + w_p[i]:
-            copy.wait_send()
+        for g in range(GROUPS):
+            exchange(g, o).wait()
+        if i < 2:
+            res[...] += project(o, 0, 512)
+    out[...] = (res[...] + project(2, 0, 512)).astype(BF)
+    for copy in w_x1 + w_d1 + w_x2 + w_d2 + sum(w_y + w_z + w_p, []):
+        copy.wait_send()
 
 
 def shards(tokens, w_query, w_key, w_value, omega, w_out):
@@ -378,7 +445,7 @@
         in_specs=[pl.BlockSpec(memory_space=pltpu.HBM)] * 6,
         out_specs=pl.BlockSpec(memory_space=pltpu.VMEM),
         scratch_shapes=[
-            V((1024, 2048), BF), V((2048, 512), BF), V((GROUPS, 2048, NH * 256), BF), V((128, 256), F32),
+            V((1024, 2048), BF), V((2, 2048, 256), BF), V((GROUPS, 2048, NH * 256), BF), V((128, 256), F32),
             V((4, 512, 2048), BF), V((1024, 1024), BF), V((1024, 1024), BF), V((1024, 512), BF),
             V((512, 256), BF), V((2,) + whole, F32), V((4, 4, 160, 256), BF),
             V((4, 1024, 256), F32), V((CHUNK, 2048), F32),
@@ -386,12 +453,12 @@
             V(part, BF), V((3,) + part, BF), V((2,) + part, BF), V((3,) + part, BF),
             V(part, F32), V(part, F32), V(part, F32),
             V(whole, BF), V((2,) + whole, BF), V((4, 256, 256), BF),
-            V((4, GROUPS, CHUNK, NH * 128), BF), V((3, GROUPS, CHUNK, NH * 128), BF),
-            dma((15,)), dma((GROUPS,)), dma((GROUPS,)),
+            V((4, CHUNK, 512), BF), V((3, CHUNK, 512), BF),
+            dma((16,)), dma((GROUPS,)), dma((GROUPS,)),
             dma((GROUPS, 3)), dma((GROUPS, 3)), dma((GROUPS, 3)), dma((GROUPS, 3)),
             dma((GROUPS, 3)), dma((GROUPS, 3)), dma((GROUPS, 3)), dma((GROUPS, 3)),
             dma((GROUPS,)), dma((GROUPS,)), dma((GROUPS, 3)), dma((GROUPS, 3)),
-            dma((3,)), dma((3,)), dma((3, 2)), dma((3, 2)), dma((3, 2)), dma((3, 2)), dma((3, 5)), dma((3, 5)),
+            dma((4, 3, 2)), dma((4, 3, 2)), dma((3, 6)), dma((3, 6)),
         ],
         compiler_params=pltpu.CompilerParams(
             collective_id=0, has_side_effects=True, vmem_limit_bytes=42 << 20

time: 52.8 us -> 42.5 us (0.80)
  Pallas kernels: 51.7 us -> 41.4 us
    pallas_call x1, Pallas kernels: 51.7 us -> 41.4 us  [shards(): pl.pallas_call(kernel, out_shape=jax.ShapeDtypeStruct((CHUNK, 2048), BF),...]
where the time goes in v3:
time: 42.5 us; the launch traced here: 42.4 us
  Pallas kernels  41.4 us (97%)
  local copies, waits for them, and re-layouts  0.97 us (2%)
    pallas_call x1, Pallas kernels, shards(): pl.pallas_call(kernel, out_shape=jax.ShapeDtypeStruct((CHUNK, 2048), BF),...  41.4 us
    unnamed x1, local copies, waits for them, and re-layouts  0.97 us

profile of v3, /device:TPU:1, one launch (start us, length us, event | category | flops | bytes accessed | tf_op | source)
XLA Modules:
  0.0 42.4 jit_solution(12043196588859137043)
XLA Ops:
  0.0 41.4 %causal_linear.1 = bf16[256,2048]{1,0:T(8,128)(2,1)S(1)} custom-call(bf16[1024,2048]{1,0:T(8,128)(2,1)} %tok.1, bf16[2048,512]{1,0:T(8,128)(2,1)} %wq.1, bf16[2048,512]{1,0:T(8,128)(2,1)} %wk.1, bf16[2048,512]{1,0:T(8,128)(2,1)} %wv.1, f32[128,256]{1,0:T(8,128)} %om.1, bf16[512,2048]{1,0:T(8,128)(2,1)} %wo.1), custom_call_target="tpu_custom_call" | custom-call | tf_op jit(solution)/shard_map/causal_linear/pallas_call | solution.py:442
  41.4 1.0 %copy.8 = bf16[256,2048]{1,0:T(8,128)(2,1)} copy(bf16[256,2048]{1,0:T(8,128)(2,1)S(1)} %causal_linear.1) | data formatting | bytes 2097152

commit v4 on v3

--- a/solution.py
+++ b/solution.py
@@ -384,52 +384,57 @@
     start2(1)
     start1(3)
     step(2)
+    w_first(0)
     start3(0)
     insides(0)
     start2(2)
     w_along_head_direct(0)
     w_along_head_direct(1)
     combine(0)
-    for i in range(2):
-        w_first(i)
-        w_p[i][0].start()
-        w_p[i][5].start()
+    w_first(1)
     insides(1)
     start3(1)
     start2(3)
+    step(2)
     w_first(2)
-    step(2)
     combine(1)
-    step(2)
-    w_p[2][0].start()
+    for i in range(2):
+        w_p[i][0].start()
+        w_p[i][5].start()
+    step(2)
+    w_second(0)
     insides(2)
     start3(2)
     insides(3)
-    w_second(0)
-    w_second(1)
     combine(2)
     start3(3)
     load_o.wait()
     res[...] = project(0, 0, 256)
+    w_p[2][0].start()
+    w_second(1)
     combine(3)
     w_second(2)
     for copy in w_d2:
         copy.wait_recv()
     w_p[2][5].start()
     w_third(0)
+    res[...] += project(0, 256, 512)
     w_third(1)
-    res[...] += project(0, 256, 512)
     for i in range(3):
         o = (1, 3, 2)[i]
-        if i == 0:
+        if i == 1:
             w_third(2)
         for copy in w_p[i]:
             copy.wait_recv()
-        for g in range(GROUPS):
+        for g in range(2):
             exchange(g, o).wait()
-        if i < 2:
-            res[...] += project(o, 0, 512)
-    out[...] = (res[...] + project(2, 0, 512)).astype(BF)
+        res[...] += project(o, 0, 256)
+    for o in (1, 3, 2):
+        for g in range(2, 4):
+            exchange(g, o).wait()
+        if o != 2:
+            res[...] += project(o, 256, 512)
+    out[...] = (res[...] + project(2, 256, 512)).astype(BF)
     for copy in w_x1 + w_d1 + w_x2 + w_d2 + sum(w_y + w_z + w_p, []):
         copy.wait_send()
 

time: 42.5 us -> 40.8 us (0.960)
  Pallas kernels: 41.4 us -> 39.7 us
    pallas_call x1, Pallas kernels: 41.4 us -> 39.7 us  [shards(): pl.pallas_call(kernel, out_shape=jax.ShapeDtypeStruct((CHUNK, 2048), BF),...]
where the time goes in v4:
time: 40.8 us; the launch traced here: 40.7 us
  Pallas kernels  39.7 us (97%)
  local copies, waits for them, and re-layouts  0.97 us (2%)
    pallas_call x1, Pallas kernels, shards(): pl.pallas_call(kernel, out_shape=jax.ShapeDtypeStruct((CHUNK, 2048), BF),...  39.7 us
    unnamed x1, local copies, waits for them, and re-layouts  0.97 us

profile of v4, /device:TPU:1, one launch (start us, length us, event | category | flops | bytes accessed | tf_op | source)
XLA Modules:
  0.0 40.7 jit_solution(3446792709970939763)
XLA Ops:
  0.0 39.7 %causal_linear.1 = bf16[256,2048]{1,0:T(8,128)(2,1)S(1)} custom-call(bf16[1024,2048]{1,0:T(8,128)(2,1)} %tok.1, bf16[2048,512]{1,0:T(8,128)(2,1)} %wq.1, bf16[2048,512]{1,0:T(8,128)(2,1)} %wk.1, bf16[2048,512]{1,0:T(8,128)(2,1)} %wv.1, f32[128,256]{1,0:T(8,128)} %om.1, bf16[512,2048]{1,0:T(8,128)(2,1)} %wo.1), custom_call_target="tpu_custom_call" | custom-call | tf_op jit(solution)/shard_map/causal_linear/pallas_call | solution.py:447
  39.7 1.0 %copy.8 = bf16[256,2048]{1,0:T(8,128)(2,1)} copy(bf16[256,2048]{1,0:T(8,128)(2,1)S(1)} %causal_linear.1) | data formatting | bytes 2097152

commit v5 on v4

--- a/solution.py
+++ b/solution.py
@@ -71,17 +71,16 @@
             )
         )
 
-    for j in range(4):
+    load_tok.append(load(tok.at[rows_of(0)], tokv.at[rows_of(0)], 1))
+    load_group(0)
+    for j in range(1, 4):
         load_tok.append(load(tok.at[rows_of(j)], tokv.at[rows_of(j)], 1 + j))
-        if j == 0:
-            load_group(0)
     load_q = []
 
     barrier = pltpu.get_barrier_semaphore()
     for to in [partner] + ydev + zdev + xdev:
         pl.semaphore_signal(barrier, inc=1, device_id=to, device_id_type=MESH)
 
-    run[...] = jnp.zeros_like(run)
     for copy in [load_tok[0], *load_kv[0]]:
         copy.wait()
     held = [dot(tokv[rows_of(0)], wkv[0])]
@@ -190,9 +189,12 @@
             state = dot(jnp.concatenate([turned[:64], norm, turned[64:], norm], axis=0), feat)
             for a in range(2):
                 for l in range(2):
-                    so_far = run[l, h, a]
-                    sloc[j, h, a * 80 : a * 80 + 80, l * 128 : (l + 1) * 128] = so_far.astype(BF)
-                    run[l, h, a] = so_far + state[a * 80 : a * 80 + 80, l * 128 : (l + 1) * 128]
+                    part = state[a * 80 : a * 80 + 80, l * 128 : (l + 1) * 128]
+                    if j > 0:
+                        so_far = run[l, h, a]
+                        sloc[j, h, a * 80 : a * 80 + 80, l * 128 : (l + 1) * 128] = so_far.astype(BF)
+                        part = so_far + part
+                    run[l, h, a] = part
 
     causal = lax.broadcasted_iota(jnp.int32, (CHUNK, CHUNK), 0) >= lax.broadcasted_iota(
         jnp.int32, (CHUNK, CHUNK), 1

time: 40.8 us -> 40.8 us (level)
  no operation moved by 1% of the time
where the time goes in v5:
time: 40.8 us; the launch traced here: 40.7 us
  Pallas kernels  39.7 us (97%)
  local copies, waits for them, and re-layouts  0.97 us (2%)
    pallas_call x1, Pallas kernels, shards(): pl.pallas_call(kernel, out_shape=jax.ShapeDtypeStruct((CHUNK, 2048), BF),...  39.7 us
    unnamed x1, local copies, waits for them, and re-layouts  0.97 us

profile of v5, /device:TPU:1, one launch (start us, length us, event | category | flops | bytes accessed | tf_op | source)
XLA Modules:
  0.0 40.7 jit_solution(12237012580897441562)
XLA Ops:
  0.0 39.7 %causal_linear.1 = bf16[256,2048]{1,0:T(8,128)(2,1)S(1)} custom-call(bf16[1024,2048]{1,0:T(8,128)(2,1)} %tok.1, bf16[2048,512]{1,0:T(8,128)(2,1)} %wq.1, bf16[2048,512]{1,0:T(8,128)(2,1)} %wk.1, bf16[2048,512]{1,0:T(8,128)(2,1)} %wv.1, f32[128,256]{1,0:T(8,128)} %om.1, bf16[512,2048]{1,0:T(8,128)(2,1)} %wo.1), custom_call_target="tpu_custom_call" | custom-call | tf_op jit(solution)/shard_map/causal_linear/pallas_call | solution.py:449
  39.7 1.0 %copy.8 = bf16[256,2048]{1,0:T(8,128)(2,1)} copy(bf16[256,2048]{1,0:T(8,128)(2,1)S(1)} %causal_linear.1) | data formatting | bytes 2097152

commit v6 on v5

--- a/solution.py
+++ b/solution.py
@@ -388,10 +388,10 @@
     step(2)
     w_first(0)
     start3(0)
+    w_along_head_direct(0)
+    w_along_head_direct(1)
     insides(0)
     start2(2)
-    w_along_head_direct(0)
-    w_along_head_direct(1)
     combine(0)
     w_first(1)
     insides(1)
@@ -430,13 +430,16 @@
             copy.wait_recv()
         for g in range(2):
             exchange(g, o).wait()
-        res[...] += project(o, 0, 256)
-    for o in (1, 3, 2):
-        for g in range(2, 4):
-            exchange(g, o).wait()
-        if o != 2:
-            res[...] += project(o, 256, 512)
-    out[...] = (res[...] + project(2, 256, 512)).astype(BF)
+        if i < 2:
+            res[...] += project(o, 0, 256)
+        if i == 1:
+            for near in (1, 3):
+                for g in range(2, 4):
+                    exchange(g, near).wait()
+                res[...] += project(near, 256, 512)
+    for g in range(2, 4):
+        exchange(g, 2).wait()
+    out[...] = (res[...] + project(2, 0, 512)).astype(BF)
     for copy in w_x1 + w_d1 + w_x2 + w_d2 + sum(w_y + w_z + w_p, []):
         copy.wait_send()
 

time: 40.8 us -> 40.6 us (level)
  no operation moved by 1% of the time
where the time goes in v6:
time: 40.6 us; the launch traced here: 40.5 us
  Pallas kernels  39.6 us (98%)
  local copies, waits for them, and re-layouts  0.97 us (2%)
    pallas_call x1, Pallas kernels, shards(): pl.pallas_call(kernel, out_shape=jax.ShapeDtypeStruct((CHUNK, 2048), BF),...  39.6 us
    unnamed x1, local copies, waits for them, and re-layouts  0.97 us

profile of v6, /device:TPU:1, one launch (start us, length us, event | category | flops | bytes accessed | tf_op | source)
XLA Modules:
  0.0 40.5 jit_solution(7805623147189811709)
XLA Ops:
  0.0 39.6 %causal_linear.1 = bf16[256,2048]{1,0:T(8,128)(2,1)S(1)} custom-call(bf16[1024,2048]{1,0:T(8,128)(2,1)} %tok.1, bf16[2048,512]{1,0:T(8,128)(2,1)} %wq.1, bf16[2048,512]{1,0:T(8,128)(2,1)} %wk.1, bf16[2048,512]{1,0:T(8,128)(2,1)} %wv.1, f32[128,256]{1,0:T(8,128)} %om.1, bf16[512,2048]{1,0:T(8,128)(2,1)} %wo.1), custom_call_target="tpu_custom_call" | custom-call | tf_op jit(solution)/shard_map/causal_linear/pallas_call | solution.py:452
  39.6 1.0 %copy.8 = bf16[256,2048]{1,0:T(8,128)(2,1)} copy(bf16[256,2048]{1,0:T(8,128)(2,1)S(1)} %causal_linear.1) | data formatting | bytes 2097152

commit v7 on v6

--- a/solution.py
+++ b/solution.py
@@ -409,11 +409,11 @@
     start3(2)
     insides(3)
     combine(2)
+    w_second(1)
     start3(3)
     load_o.wait()
     res[...] = project(0, 0, 256)
     w_p[2][0].start()
-    w_second(1)
     combine(3)
     w_second(2)
     for copy in w_d2:

time: 40.6 us -> 40.6 us (level)
  no operation moved by 1% of the time
where the time goes in v7:
time: 40.6 us; the launch traced here: 40.5 us
  Pallas kernels  39.6 us (98%)
  local copies, waits for them, and re-layouts  0.97 us (2%)
    pallas_call x1, Pallas kernels, shards(): pl.pallas_call(kernel, out_shape=jax.ShapeDtypeStruct((CHUNK, 2048), BF),...  39.6 us
    unnamed x1, local copies, waits for them, and re-layouts  0.97 us

profile of v7, /device:TPU:1, one launch (start us, length us, event | category | flops | bytes accessed | tf_op | source)
XLA Modules:
  0.0 40.5 jit_solution(4291273433141248927)
XLA Ops:
  0.0 39.6 %causal_linear.1 = bf16[256,2048]{1,0:T(8,128)(2,1)S(1)} custom-call(bf16[1024,2048]{1,0:T(8,128)(2,1)} %tok.1, bf16[2048,512]{1,0:T(8,128)(2,1)} %wq.1, bf16[2048,512]{1,0:T(8,128)(2,1)} %wk.1, bf16[2048,512]{1,0:T(8,128)(2,1)} %wv.1, f32[128,256]{1,0:T(8,128)} %om.1, bf16[512,2048]{1,0:T(8,128)(2,1)} %wo.1), custom_call_target="tpu_custom_call" | custom-call | tf_op jit(solution)/shard_map/causal_linear/pallas_call | solution.py:452
  39.6 1.0 %copy.8 = bf16[256,2048]{1,0:T(8,128)(2,1)} copy(bf16[256,2048]{1,0:T(8,128)(2,1)S(1)} %causal_linear.1) | data formatting | bytes 2097152
